TPU v7x, 512 devices: a whole 4x4x16 slice. The times are simulated.
512 devices in a mesh: dp: 32 (over z, core), shard: 16 (over y, x).
Axes of the slice: x: 4, y: 4, z: 16, core: 2. Of those that a mesh axis runs over, the one named last changes fastest.
Arguments:
- tokens: bfloat16 [196608, 512], P(('dp', 'shard')), may hold values from -24 to 24
- w_proj: bfloat16 [512, 2048], P(None, 'shard'), may hold values from -0.25 to 0.25
- w_out: bfloat16 [512, 512], replicated, may hold values from -0.25 to 0.25
- item_rows: bfloat16 [16384, 512], P('shard'), may hold values from -1.5 to 1.5
- lengths: int32 [512, 4], P(('dp', 'shard')), may hold values from 1 to 192, 384 in all within a row
- target_owner: int32 [196608, 1], P(('dp', 'shard')), may hold values from 0 to 15; in each aligned block of 384 rows (0 to 383, 384 to 767, ...) at most 48 rows name the same one
- target_row: int32 [196608], P(('dp', 'shard')), may hold values from 0 to 1023
- negative_rows: int32 [1024], P('shard'), may hold values from 0 to 1023
Outputs:
- grad_tokens: bfloat16 [196608, 512], P(('dp', 'shard'))
- weight_grads: float32 [512, 512], replicated
- item_grads: float32 [16384, 512], P('shard')
Inputs may be any that keep to these rules, and one draw needn't show every extreme that they name: `target_owner`: in the rows of one device no owner is named more than 48 times, a bound that some block reaches.
All inputs are finite; a program needn't handle non-finite values.
Results may differ from a plain program's by a relative error of at most 0.02.
Values may be sent and summed in bfloat16 or wider, within the bound.
No kernel may reach another device: no remote copies, remote signals or barrier semaphores. Data moves between devices by JAX's collectives and lax.ppermute only.
A program may use at most 64 MiB of HBM per device.

v0:
```python
import jax
import jax.numpy as jnp
from jax import lax
from jax.sharding import PartitionSpec as P

D = 512
HEADS = 4
DH = 128
MAXLEN = 192
epsilon = 1e-06
logit_divisor = 0.015625
loss_scale = 512.0


def reduce_last_dimension(operand, other_side):
    return lax.dot_general(
        operand, other_side, (((1,), (1,)), ((), ())), preferred_element_type=jnp.float32
    )


def contract_first(operand, other_side):
    return lax.dot_general(
        operand, other_side, (((0,), (0,)), ((), ())), preferred_element_type=jnp.float32
    )


def silu_slope(values):
    sigmoid = jax.nn.sigmoid(values)
    return sigmoid * (1.0 + values * (1.0 - sigmoid))


def history_mask(lengths_row, rows_count):
    history_ends = jnp.cumsum(lengths_row)
    positions = jnp.arange(rows_count, dtype=jnp.int32)
    history_ids = jnp.sum((positions[:, None] >= history_ends[None, :-1]).astype(jnp.int32), axis=1)
    visible = (history_ids[:, None] == history_ids[None, :]) & (
        positions[None, :] <= positions[:, None]
    )
    return jnp.where(visible, 1.0, 0.0).astype(jnp.float32)


def head_columns(activated, section, head_index):
    first_col = section * D + head_index * DH
    return activated[:, first_col : first_col + DH]


def head_scores(queries, key_rows):
    return reduce_last_dimension(queries, key_rows) * DH ** (-0.5)


def head_weights(scores, visible):
    return (jax.nn.silu(scores) * visible * (1.0 / MAXLEN)).astype(jnp.bfloat16)


def forward_layer(tokens, project, w_out, visible):
    wide_tokens = tokens.astype(jnp.float32)
    input_scale = lax.rsqrt(jnp.mean(wide_tokens * wide_tokens, axis=1, keepdims=True) + epsilon)
    normed = (wide_tokens * input_scale).astype(jnp.bfloat16)
    pre_act = project(normed)
    activated = lax.optimization_barrier(jax.nn.silu(pre_act).astype(jnp.bfloat16))
    heads_out = []
    for head_index in range(HEADS):
        queries = head_columns(activated, 2, head_index)
        key_rows = head_columns(activated, 3, head_index)
        value_rows = head_columns(activated, 1, head_index)
        weights = head_weights(head_scores(queries, key_rows), visible)
        heads_out.append(jnp.dot(weights, value_rows, preferred_element_type=jnp.float32))
    joined = lax.optimization_barrier(jnp.concatenate(heads_out, axis=1).astype(jnp.bfloat16))
    joined_wide = joined.astype(jnp.float32)
    middle_scale = lax.rsqrt(jnp.mean(joined_wide * joined_wide, axis=1, keepdims=True) + epsilon)
    gate_wide = activated[:, :D].astype(jnp.float32)
    gated = (joined_wide * middle_scale * gate_wide).astype(jnp.bfloat16)
    layer_out = wide_tokens + jnp.dot(gated, w_out, preferred_element_type=jnp.float32)
    return (layer_out, (wide_tokens, input_scale, pre_act, activated, joined, middle_scale, gated))


def loss_head(layer_out, clicked_product_vectors, sampled_decoys):
    out_scale = lax.rsqrt(jnp.sum(layer_out * layer_out, axis=1, keepdims=True) + epsilon)
    normalized_example_vectors = lax.optimization_barrier(
        (layer_out * out_scale).astype(jnp.bfloat16)
    )
    normalized_complete_embedding = normalized_example_vectors.astype(jnp.float32)
    correct_logit_entry = (
        jnp.sum(normalized_complete_embedding * clicked_product_vectors.astype(jnp.float32), axis=1)
        / logit_divisor
    )
    decoy_logit_entries = (
        reduce_last_dimension(normalized_example_vectors, sampled_decoys) / logit_divisor
    )
    target_exp = jnp.exp(correct_logit_entry)
    negative_exp = jnp.exp(decoy_logit_entries)
    totals = target_exp + jnp.sum(negative_exp, axis=1)
    target_prob = target_exp / totals
    negative_probs = (loss_scale * negative_exp / totals[:, None]).astype(jnp.bfloat16)
    target_coef = (loss_scale * (target_prob - 1.0))[:, None]
    grad_unit = target_coef * clicked_product_vectors.astype(jnp.float32) + jnp.dot(
        negative_probs, sampled_decoys, preferred_element_type=jnp.float32
    )
    grad_out = out_scale * grad_unit - layer_out * out_scale**3 * jnp.sum(
        layer_out * grad_unit, axis=1, keepdims=True
    )
    grad_target = target_coef * normalized_complete_embedding
    return (grad_out, grad_target, negative_probs, normalized_example_vectors)


def backward_layer(grad_out, saved_state, project_back, w_out, visible):
    wide_tokens, input_scale, pre_act, activated, joined, middle_scale, gated = saved_state
    grad_out_b = grad_out.astype(jnp.bfloat16)
    weight_part = contract_first(gated, grad_out_b)
    grad_gated = reduce_last_dimension(grad_out_b, w_out)
    joined_wide = joined.astype(jnp.float32)
    gate_wide = activated[:, :D].astype(jnp.float32)
    grad_gate = grad_gated * joined_wide * middle_scale
    grad_norm = grad_gated * gate_wide
    grad_joined = middle_scale * grad_norm - joined_wide * middle_scale**3 * jnp.mean(
        joined_wide * grad_norm, axis=1, keepdims=True
    )
    grad_joined_b = grad_joined.astype(jnp.bfloat16)
    grad_values = []
    grad_queries = []
    grad_keys = []
    for head_index in range(HEADS):
        queries = head_columns(activated, 2, head_index)
        key_rows = head_columns(activated, 3, head_index)
        value_rows = head_columns(activated, 1, head_index)
        scores = head_scores(queries, key_rows)
        weights = head_weights(scores, visible)
        grad_head = grad_joined_b[:, head_index * DH : (head_index + 1) * DH]
        grad_weights = reduce_last_dimension(grad_head, value_rows)
        grad_values.append(contract_first(weights, grad_head))
        grad_scores = (
            grad_weights * visible * (1.0 / MAXLEN) * silu_slope(scores) * DH ** (-0.5)
        ).astype(jnp.bfloat16)
        grad_queries.append(jnp.dot(grad_scores, key_rows, preferred_element_type=jnp.float32))
        grad_keys.append(contract_first(grad_scores, queries))
    grad_act = jnp.concatenate([grad_gate] + grad_values + grad_queries + grad_keys, axis=1)
    grad_pre = (grad_act * silu_slope(pre_act)).astype(jnp.bfloat16)
    grad_normed = project_back(grad_pre)
    grad_input = input_scale * grad_normed - wide_tokens * input_scale**3 * jnp.mean(
        wide_tokens * grad_normed, axis=1, keepdims=True
    )
    return ((grad_out + grad_input).astype(jnp.bfloat16), weight_part)


def finish_rows(grad_items, rows_wide):
    item_scale = lax.rsqrt(jnp.sum(rows_wide * rows_wide, axis=1, keepdims=True) + epsilon)
    return (
        item_scale * grad_items
        - rows_wide * item_scale**3 * jnp.sum(rows_wide * grad_items, axis=1, keepdims=True)
    ) / loss_scale


def shards(tokens, w_proj, w_out, item_rows, lengths, target_owner, target_row, negative_rows):
    tok_rows = tokens.shape[0]
    model_width = tokens.shape[1]
    shard_count = lax.axis_size("shard")
    capacity = 2 * tok_rows // shard_count
    visible = history_mask(lengths[0], tok_rows)

    def project(normed):
        return jnp.dot(
            normed,
            lax.all_gather(w_proj, "shard", axis=1, tiled=True),
            preferred_element_type=jnp.float32,
        )

    def project_back(grad_pre):
        return reduce_last_dimension(grad_pre, lax.all_gather(w_proj, "shard", axis=1, tiled=True))

    rows_wide = item_rows.astype(jnp.float32)
    item_scale = lax.rsqrt(jnp.sum(rows_wide * rows_wide, axis=1, keepdims=True) + epsilon)
    unit_items = (rows_wide * item_scale).astype(jnp.bfloat16)
    owners = target_owner[:, 0]
    owner_hits = (owners[:, None] == jnp.arange(shard_count, dtype=jnp.int32)[None, :]).astype(
        jnp.int32
    )
    earlier = jnp.cumsum(owner_hits, axis=0) - owner_hits
    slot_index = jnp.sum(earlier * owner_hits, axis=1)
    position = owners * capacity + slot_index
    requests = jnp.zeros((shard_count * capacity,), jnp.int32).at[position].set(target_row)
    asked_rows = lax.all_to_all(
        requests.reshape(shard_count, capacity), "shard", split_axis=0, concat_axis=0, tiled=True
    )
    asked_flat = asked_rows.reshape(-1)
    served = jnp.take(unit_items, asked_flat, axis=0).reshape(shard_count, capacity, model_width)
    fetched = lax.all_to_all(served, "shard", split_axis=0, concat_axis=0, tiled=True)
    clicked_product_vectors = jnp.take(
        fetched.reshape(shard_count * capacity, model_width), position, axis=0
    )
    sampled_decoys = lax.all_gather(
        jnp.take(unit_items, negative_rows, axis=0), "shard", axis=0, tiled=True
    )
    layer_out, saved_state = forward_layer(tokens, project, w_out, visible)
    grad_out, grad_target, negative_probs, normalized_example_vectors = loss_head(
        layer_out, clicked_product_vectors, sampled_decoys
    )
    grad_tokens, weight_part = backward_layer(grad_out, saved_state, project_back, w_out, visible)
    outgoing = (
        jnp.zeros((shard_count * capacity, model_width), jnp.float32).at[position].set(grad_target)
    )
    returned = lax.all_to_all(
        outgoing.reshape(shard_count, capacity, model_width).astype(jnp.bfloat16),
        "shard",
        split_axis=0,
        concat_axis=0,
        tiled=True,
    ).astype(jnp.float32)
    grad_items = (
        jnp.zeros((item_rows.shape[0], model_width), jnp.float32)
        .at[asked_flat]
        .add(returned.reshape(-1, model_width))
    )
    own_negatives = lax.psum_scatter(
        contract_first(negative_probs, normalized_example_vectors).astype(jnp.bfloat16),
        "shard",
        scatter_dimension=0,
        tiled=True,
    ).astype(jnp.float32)
    grad_items = grad_items.at[negative_rows].add(own_negatives)
    grad_items = lax.psum(grad_items.astype(jnp.bfloat16), "dp").astype(jnp.float32)
    item_grads = finish_rows(grad_items, rows_wide)
    weight_grads = lax.psum(weight_part, ("dp", "shard")) / loss_scale
    return (grad_tokens, weight_grads, item_grads)


def solution(mesh):
    in_specs = (
        P(("dp", "shard"), None),
        P(None, "shard"),
        P(),
        P("shard", None),
        P(("dp", "shard"), None),
        P(("dp", "shard"), None),
        P(("dp", "shard")),
        P("shard"),
    )
    out_specs = (P(("dp", "shard"), None), P(), P("shard", None))
    return jax.shard_map(shards, mesh=mesh, in_specs=in_specs, out_specs=out_specs, check_vma=False)
```

profile of v0, /device:TPU:1, one launch (start us, length us, event | category | flops | bytes accessed | tf_op | source)
XLA Modules:
  0.0 947.1 jit_solution(13287930997406279915)
XLA Ops:
  7.2 0.7 all-gather.3.cloned.1.call-update
  7.9 0.7 reduce
  8.6 0.9 reduce-window.11
  9.9 1.2 and_reduce_fusion
  11.1 3.1 scatter_custom_fusion
  14.2 0.7 all_to_all.12
  14.9 7.6 all-to-all-start
  22.4 0.8 reduce-window.10
  23.3 1.2 fusion.29
  24.4 1.5 fusion.2
  25.9 0.7 compare_select_fusion.3
  27.0 1.8 all-to-all-done
  29.3 0.7 reduce.12
  30.1 2.7 gather_fusion
  32.9 1.1 broadcast_select_fusion
  33.9 4.9 all-to-all-start.1
  38.9 0.6 multiply_multiply_fusion.1
  39.5 0.7 gather_fusion.2
  40.2 0.7 broadcast_select_fusion.2
  41.2 9.7 %all-to-all-done.1 = bf16[16,48,512]{2,1,0:T(8,128)(2,1)S(1)} async-done(((bf16[16,48,512]{2,1,0:T(8,128)(2,1)}), bf16[16,48,512]{2,1,0:T(8,128)(2,1)S(1)}, u32[]{:S(2)}, u32[]{:S(2)}) %all-to-all-start.1) | async-done | bytes 786464 | tf_op jit(solution)/shard_map/all_to_all | solution.py:186
  50.9 2.6 gather_fusion.1
  53.4 26.8 %all-gather.3.cloned.1.call-done = bf16[512,2048]{1,0:T(8,128)(2,1)} async-done(((bf16[512,128]{1,0:T(8,128)(2,1)}), bf16[512,2048]{1,0:T(8,128)(2,1)}) %all-gather.3.cloned.1.call-update) | async-done | bytes 2097168 | tf_op jit(solution)/shard_map/all_gather | solution.py:163
  80.3 4.5 multiply_convert_fusion.1
  85.6 1.6 fusion.45
  88.5 0.6 multiply_multiply_fusion.2
  89.7 0.6 multiply_multiply_fusion.3
  90.5 0.9 fusion.28
  91.4 49.3 %all-gather.5.cloned.1.call-done = bf16[1024,512]{1,0:T(8,128)(2,1)} async-done(((bf16[64,512]{1,0:T(8,128)(2,1)}), bf16[1024,512]{1,0:T(8,128)(2,1)}) %all-gather.5.cloned.1.call-update) | async-done | bytes 1048592 | tf_op jit(solution)/shard_map/all_gather | solution.py:190
  140.7 1.9 fusion.106
  142.7 0.6 fusion.102
  143.9 1.9 convolution_convert_fusion
  145.7 2.4 multiply_reduce_fusion
  148.2 1.5 multiply_subtract_fusion
  150.4 1.2 fusion.41
  151.6 1.1 fusion.23
  152.8 1.1 fusion.22
  154.0 3.3 scatter_custom_fusion.1
  157.2 2.4 convert_element_type.136
  159.6 4.4 all-to-all-start.2
  164.4 1.7 fusion.24
  166.1 1.0 convolution_dynamic-update-slice_fusion.11
  167.1 1.0 convolution_dynamic-update-slice_fusion.10
  168.1 1.0 convolution_dynamic-update-slice_fusion.9
  169.1 1.0 convolution_dynamic-update-slice_fusion.8
  170.1 1.0 convolution_dynamic-update-slice_fusion.7
  171.0 1.0 convolution_dynamic-update-slice_fusion.6
  172.0 1.0 convolution_dynamic-update-slice_fusion.5
  173.4 1.0 convolution_dynamic-update-slice_fusion.4
  174.3 1.0 convolution_dynamic-update-slice_fusion.3
  175.3 1.0 convolution_dynamic-update-slice_fusion.2
  176.3 1.0 convolution_dynamic-update-slice_fusion.1
  177.3 1.0 convolution_dynamic-update-slice_fusion
  178.3 1.5 fusion.57
  179.9 5.8 fusion.35
  186.2 8.5 scatter_custom_fusion.2
  194.8 48.9 %reduce-scatter.2.cloned.1.call-done = bf16[64,512]{1,0:T(8,128)(2,1)} async-done(((bf16[1024,512]{1,0:T(8,128)(2,1)}), bf16[64,512]{1,0:T(8,128)(2,1)}) %reduce-scatter.2.cloned.1.call-update) | async-done | bytes 65552 | tf_op jit(solution)/shard_map/reduce_scatter | solution.py:213
  243.6 4.1 scatter_custom_fusion.3
  247.8 2.8 convert_element_type.140
  250.7 1.7 fusion.34
  252.4 472.2 %all-reduce.3.cloned.1.call-done = f32[512,512]{1,0:T(8,128)} async-done(((f32[512,512]{1,0:T(8,128)}), f32[512,512]{1,0:T(8,128)}) %all-reduce.3.cloned.1.call-update) | async-done | bytes 1048592 | tf_op jit(solution)/shard_map/psum | solution.py:222
  724.5 2.3 broadcast_multiply_fusion
  726.8 210.2 %all-reduce.5.cloned.1.call-done = bf16[1024,512]{1,0:T(8,128)(2,1)} async-done(((bf16[1024,512]{1,0:T(8,128)(2,1)}), bf16[1024,512]{1,0:T(8,128)(2,1)}) %all-reduce.5.cloned.1.call-update) | async-done | bytes 1048592 | tf_op jit(solution)/shard_map/psum | solution.py:220
  937.0 1.7 fusion.5
  938.7 1.9 fusion.1
  (135 shorter events, 7.2 us)
Async XLA Ops:
  7.2 81.9 %copy-start = (bf16[512,512]{1,0:T(8,128)(2,1)S(1)}, bf16[512,512]{1,0:T(8,128)(2,1)}, u32[]{:S(2)}) copy-start(bf16[512,512]{1,0:T(8,128)(2,1)} %param.10) | copy-start | bytes 1572868
  7.2 19.4 %copy-start.1 = (bf16[1024,512]{1,0:T(8,128)(2,1)S(1)}, bf16[1024,512]{1,0:T(8,128)(2,1)}, u32[]{:S(2)}) copy-start(bf16[1024,512]{1,0:T(8,128)(2,1)} %param.11) | copy-start | bytes 3145732
  7.2 73.1 %all-gather.3.cloned.1.call-start = ((), (), s32[]{:S(2)}) async-start(), calls=%async_computation.4 | async-start | bytes 2228224 | tf_op jit(solution)/shard_map/all_gather | solution.py:163
  11.1 27.7 %copy-start.35 = (s32[384]{0:T(512)}, s32[384]{0:T(512)S(1)}, u32[]{:S(2)}) copy-start(s32[384]{0:T(512)S(1)} %reduce.4) | copy-start | bytes 4612
  14.9 13.9 %all-to-all-start = ((s32[16,1,48]{2,1,0:T(1,128)}), s32[16,1,48]{2,1,0:T(1,128)S(1)}, u32[]{:S(2)}, u32[]{:S(2)}) async-start(s32[16,1,48]{2,1,0:T(1,128)} %all_to_all.12), calls=%async_computation | async-start | bytes 16384 | tf_op jit(solution)/shard_map/all_to_all | solution.py:181
  26.6 6.2 copy-start.45
  27.0 58.6 %copy-start.40 = (s32[384]{0:T(512)}, s32[384]{0:T(512)S(1)}, u32[]{:S(2)}) copy-start(s32[384]{0:T(512)S(1)} %convert_reduce_fusion) | copy-start | bytes 4612
  30.1 2.7 copy-start.31
  32.8 6.0 copy-start.46
  33.9 17.0 %all-to-all-start.1 = ((bf16[16,48,512]{2,1,0:T(8,128)(2,1)}), bf16[16,48,512]{2,1,0:T(8,128)(2,1)S(1)}, u32[]{:S(2)}, u32[]{:S(2)}) async-start(bf16[16,48,512]{2,1,0:T(8,128)(2,1)} %broadcast_select_fusion), calls=%async_computation.1 | async-start | bytes 1572864 | tf_op jit(solution)/shard_map/all_to_all | solution.py:186
  38.8 101.9 %all-gather.5.cloned.1.call-start = ((), (), s32[]{:S(2)}) async-start(), calls=%async_computation.5 | async-start | bytes 1114112 | tf_op jit(solution)/shard_map/all_gather | solution.py:190
  39.5 40.8 %copy-start.37 = (f32[384]{0:T(512)}, f32[384]{0:T(512)S(1)}, u32[]{:S(2)}) copy-start(f32[384]{0:T(512)S(1)} %get-tuple-element.12) | copy-start | bytes 4612
  40.2 40.1 %copy-start.11 = (bf16[384,512]{1,0:T(8,128)(2,1)S(1)}, bf16[384,512]{1,0:T(8,128)(2,1)}, u32[]{:S(2)}) copy-start(bf16[384,512]{1,0:T(8,128)(2,1)} %param.8) | copy-start | bytes 1179652
  40.9 202.7 %reduce-scatter.2.cloned.1.call-start = ((), (), s32[]{:S(2)}) async-start(), calls=%async_computation.7 | async-start | bytes 1114112 | tf_op jit(solution)/shard_map/reduce_scatter | solution.py:213
  84.7 4.4 copy-start.2
  85.0 2.2 copy-start.25
  85.3 1.9 copy-start.27
  85.6 1.6 copy-start.29
  87.2 2.4 copy-start.16
  87.2 2.4 copy-start.18
  87.2 2.4 copy-start.20
  87.2 2.4 copy-start.22
  87.2 1.9 copy-start.12
  88.3 2.2 copy-start.10
  88.3 2.1 copy-start.44
  89.7 56.1 %copy-start.6 = (f32[384,512]{1,0:T(8,128)}, f32[384,512]{1,0:T(8,128)S(1)}, u32[]{:S(2)}) copy-start(f32[384,512]{1,0:T(8,128)S(1)} %get-tuple-element.25) | copy-start | bytes 2359300
  140.7 2.0 copy-start.34
  142.6 1.2 copy-start.9
  143.3 0.6 copy-start.43
  145.7 2.4 copy-start.39
  148.2 1.6 copy-start.3
  148.2 2.2 copy-start.32
  150.3 1.2 copy-start.30
  150.3 1.2 copy-start.41
  151.6 1.1 copy-start.7
  151.6 1.2 copy-start.28
  152.8 1.2 copy-start.33
  157.2 7.1 copy-start.42
  159.6 26.6 %all-to-all-start.2 = ((bf16[16,48,512]{2,1,0:T(8,128)(2,1)}), bf16[16,48,512]{2,1,0:T(8,128)(2,1)S(1)}, u32[]{:S(2)}, u32[]{:S(2)}) async-start(bf16[16,48,512]{2,1,0:T(8,128)(2,1)} %bitcast.59), calls=%async_computation.2 | async-start | bytes 1572864 | tf_op jit(solution)/shard_map/all_to_all | solution.py:201
  164.0 560.5 %all-reduce.3.cloned.1.call-start = ((), (), s32[]{:S(2)}) async-start(), calls=%async_computation.6 | async-start | bytes 2097152 | tf_op jit(solution)/shard_map/psum | solution.py:222
  164.3 1.8 copy-start.8
  164.3 1.8 copy-start.23
  164.3 2.8 copy-start.21
  164.3 3.8 copy-start.19
  164.3 4.7 copy-start.17
  166.0 4.0 copy-start.4
  166.1 5.0 copy-start.15
  166.1 5.9 copy-start.14
  166.1 6.9 copy-start.26
  179.8 757.2 %all-reduce.5.cloned.1.call-start = ((), (), s32[]{:S(2)}) async-start(), calls=%async_computation.8 | async-start | bytes 2097152 | tf_op jit(solution)/shard_map/psum | solution.py:220
  247.8 2.9 copy-start.13
  247.8 2.9 copy-start.24
  247.8 2.9 copy-start.36
  247.8 2.9 copy-start.38
  937.0 1.7 copy-start.5
Sparse Core Ops, SparseCore 0:
  11.0 69.2 all-gather.2
  83.8 56.8 all-gather.4
  154.1 89.5 reduce-scatter.1
  249.5 474.9 all-reduce.2
  726.7 210.2 all-reduce.4
where the time goes:
time: 948 us; the launch traced here: 947 us
  waiting for transfers between devices  820 us (86%)
  other arithmetic  45.6 us (5%)
  matrix products  38.5 us (4%)
  starting transfers between devices  17.4 us (2%)
  between operations  14.4 us (2%)
  local copies, waits for them, and re-layouts  11.5 us (1%)
    psum x1, waiting for transfers between devices, shards(): weight_grads = lax.psum(weight_part, ('dp', 'shard')) / loss_scale  472 us
    psum x1, waiting for transfers between devices, shards(): lax.psum(grad_items.astype(jnp.bfloat16), 'dp').astype(jnp.float32)  210 us
    all_gather x1, waiting for transfers between devices, shards(): lax.all_gather(jnp.take(unit_items, negative_rows, axis=0), 'shard', axis...  49.3 us
    reduce_scatter x1, waiting for transfers between devices, shards(): lax.psum_scatter(contract_first(negative_probs, normalized_example_vector...  48.9 us
    all_gather x1, waiting for transfers between devices, project(): lax.all_gather(w_proj, 'shard', axis=1, tiled=True)  26.8 us
  transfers between devices with their start and end apart: 8, of which 7 were waited for; matrix products, arithmetic and copies ran while one was open for 8% of the time, Pallas kernels for 0%

commit v1 on v0

--- a/solution.py
+++ b/solution.py
@@ -219,7 +219,7 @@
     grad_items = grad_items.at[negative_rows].add(own_negatives)
     grad_items = lax.psum(grad_items.astype(jnp.bfloat16), "dp").astype(jnp.float32)
     item_grads = finish_rows(grad_items, rows_wide)
-    weight_grads = lax.psum(weight_part, ("dp", "shard")) / loss_scale
+    weight_grads = lax.psum(lax.psum(weight_part, "dp"), "shard") / loss_scale
     return (grad_tokens, weight_grads, item_grads)
 
 

time: 948 us -> 803 us (0.85)
  waiting for transfers between devices: 820 us -> 664 us
    psum x1 -> x2, waiting for transfers between devices: 472 us -> 286 us  [shards(): weight_grads = lax.psum(lax.psum(weight_part, 'dp'), 'shard') / loss_scale]
    reduce_scatter x1, waiting for transfers between devices: 48.9 us -> 77 us  [shards(): lax.psum_scatter(contract_first(negative_probs, normalized_example_vector...]
  transfers between devices with their start and end apart: 8 -> 9, of which waited for: 7 -> 8; matrix products, arithmetic and copies ran while one was open for 8% -> 11% of each run, Pallas kernels for 0% -> 0%
where the time goes in v1:
time: 803 us; the launch traced here: 801 us
  waiting for transfers between devices  664 us (83%)
  other arithmetic  47.1 us (6%)
  matrix products  46.7 us (6%)
  starting transfers between devices  17.5 us (2%)
  between operations  14.8 us (2%)
  local copies, waits for them, and re-layouts  10.9 us (1%)
    psum x2, waiting for transfers between devices, shards(): weight_grads = lax.psum(lax.psum(weight_part, 'dp'), 'shard') / loss_scale  286 us
    psum x1, waiting for transfers between devices, shards(): lax.psum(grad_items.astype(jnp.bfloat16), 'dp').astype(jnp.float32)  214 us
    reduce_scatter x1, waiting for transfers between devices, shards(): lax.psum_scatter(contract_first(negative_probs, normalized_example_vector...  77 us
    all_gather x1, waiting for transfers between devices, shards(): lax.all_gather(jnp.take(unit_items, negative_rows, axis=0), 'shard', axis...  48.8 us
    all_gather x1, waiting for transfers between devices, project(): lax.all_gather(w_proj, 'shard', axis=1, tiled=True)  26.8 us
    dot_general x11, matrix products, reduce_last_dimension(): lax.dot_general(operand, other_side, (((1,), (1,)), ((), ())), preferred_...  17.1 us
  transfers between devices with their start and end apart: 9, of which 8 were waited for; matrix products, arithmetic and copies ran while one was open for 11% of the time, Pallas kernels for 0%

profile of v1, /device:TPU:1, one launch (start us, length us, event | category | flops | bytes accessed | tf_op | source)
XLA Modules:
  0.0 801.4 jit_solution(5489967399916307236)
XLA Ops:
  7.2 0.7 all-gather.3.cloned.1.call-update
  7.9 0.7 reduce
  8.6 0.9 reduce-window.11
  9.9 1.2 and_reduce_fusion
  11.1 3.1 scatter_custom_fusion
  14.2 0.7 all_to_all.12
  14.9 7.6 all-to-all-start
  22.5 0.8 reduce-window.10
  23.3 1.2 fusion.29
  24.5 1.5 fusion.2
  26.0 0.7 compare_select_fusion.3
  27.0 1.8 all-to-all-done
  29.4 0.7 reduce.12
  30.2 2.7 gather_fusion
  32.9 1.1 broadcast_select_fusion
  33.9 4.9 all-to-all-start.1
  39.5 0.7 gather_fusion.2
  40.2 0.7 broadcast_select_fusion.2
  41.2 9.7 %all-to-all-done.1 = bf16[16,48,512]{2,1,0:T(8,128)(2,1)S(1)} async-done(((bf16[16,48,512]{2,1,0:T(8,128)(2,1)}), bf16[16,48,512]{2,1,0:T(8,128)(2,1)S(1)}, u32[]{:S(2)}, u32[]{:S(2)}) %all-to-all-start.1) | async-done | bytes 786464 | tf_op jit(solution)/shard_map/all_to_all | solution.py:186
  50.9 2.6 gather_fusion.1
  53.5 26.8 %all-gather.3.cloned.1.call-done = bf16[512,2048]{1,0:T(8,128)(2,1)} async-done(((bf16[512,128]{1,0:T(8,128)(2,1)}), bf16[512,2048]{1,0:T(8,128)(2,1)}) %all-gather.3.cloned.1.call-update) | async-done | bytes 2097168 | tf_op jit(solution)/shard_map/all_gather | solution.py:163
  80.3 4.5 multiply_convert_fusion.1
  85.6 1.6 fusion.45
  89.7 0.6 multiply_multiply_fusion.3
  90.5 0.9 fusion.28
  91.4 48.8 %all-gather.5.cloned.1.call-done = bf16[1024,512]{1,0:T(8,128)(2,1)} async-done(((bf16[64,512]{1,0:T(8,128)(2,1)}), bf16[1024,512]{1,0:T(8,128)(2,1)}) %all-gather.5.cloned.1.call-update) | async-done | bytes 1048592 | tf_op jit(solution)/shard_map/all_gather | solution.py:190
  140.2 2.0 fusion.106
  142.3 1.4 multiply_reduce_fusion
  143.7 1.5 multiply_subtract_fusion
  145.3 1.3 fusion.42
  146.6 1.5 fusion.57
  148.8 3.3 scatter_custom_fusion.1
  152.1 2.4 convert_element_type.136
  154.5 4.4 all-to-all-start.2
  159.0 2.6 fusion.41
  161.6 1.4 fusion.23
  163.0 2.1 fusion.24
  165.2 1.0 convolution_dynamic-update-slice_fusion.11
  166.2 1.0 convolution_dynamic-update-slice_fusion.10
  167.1 1.0 convolution_dynamic-update-slice_fusion.9
  168.1 1.0 convolution_dynamic-update-slice_fusion.8
  169.1 1.9 convolution_convert_fusion
  171.3 1.9 convolution_dynamic-update-slice_fusion.7
  173.2 1.8 convolution_dynamic-update-slice_fusion.6
  175.0 1.6 fusion.22
  176.6 1.8 convolution_dynamic-update-slice_fusion.5
  178.5 1.4 fusion.21
  179.8 1.9 convolution_dynamic-update-slice_fusion.4
  181.7 1.9 convolution_dynamic-update-slice_fusion.3
  183.6 1.9 convolution_dynamic-update-slice_fusion.2
  185.5 1.9 convolution_dynamic-update-slice_fusion.1
  187.3 1.9 convolution_dynamic-update-slice_fusion
  189.2 173.8 %all-reduce.4.cloned.1.call-done = f32[512,512]{1,0:T(8,128)} async-done(((f32[512,512]{1,0:T(8,128)}), f32[512,512]{1,0:T(8,128)}) %all-reduce.4.cloned.1.call-update) | async-done | bytes 1048592 | tf_op jit(solution)/shard_map/psum | solution.py:222
  363.1 4.9 fusion.35
  368.6 8.7 %scatter_custom_fusion.2 = f32[1024,512]{1,0:T(8,128)} fusion(s32[768]{0:T(1024)} %copy-done.27, bf16[768,512]{1,0:T(8,128)(2,1)} %bitcast.8, f32[]{:T(128)} %constant.55.clone.1), kind=kCustom, calls=%fused_computation.29 | custom fusion | flops 786432 | bytes 2884096 | tf_op jit(solution)/shard_map/scatter-add | solution.py:211
  377.3 77.0 %reduce-scatter.2.cloned.1.call-done = bf16[64,512]{1,0:T(8,128)(2,1)} async-done(((bf16[1024,512]{1,0:T(8,128)(2,1)}), bf16[64,512]{1,0:T(8,128)(2,1)}) %reduce-scatter.2.cloned.1.call-update) | async-done | bytes 65552 | tf_op jit(solution)/shard_map/reduce_scatter | solution.py:213
  454.3 4.1 scatter_custom_fusion.3
  458.4 2.8 convert_element_type.140
  461.2 1.7 fusion.34
  462.9 112.3 %all-reduce.6.cloned.1.call-done = f32[512,512]{1,0:T(8,128)} async-done(((f32[512,512]{1,0:T(8,128)}), f32[512,512]{1,0:T(8,128)}) %all-reduce.6.cloned.1.call-update) | async-done | bytes 1048592 | tf_op jit(solution)/shard_map/psum | solution.py:222
  575.1 2.3 broadcast_multiply_fusion
  577.4 213.6 %all-reduce.8.cloned.1.call-done = bf16[1024,512]{1,0:T(8,128)(2,1)} async-done(((bf16[1024,512]{1,0:T(8,128)(2,1)}), bf16[1024,512]{1,0:T(8,128)(2,1)}) %all-reduce.8.cloned.1.call-update) | async-done | bytes 1048592 | tf_op jit(solution)/shard_map/psum | solution.py:220
  791.0 1.7 fusion.5
  792.7 1.9 fusion.1
  (134 shorter events, 7.4 us)
Async XLA Ops:
  7.2 82.0 %copy-start = (bf16[512,512]{1,0:T(8,128)(2,1)S(1)}, bf16[512,512]{1,0:T(8,128)(2,1)}, u32[]{:S(2)}) copy-start(bf16[512,512]{1,0:T(8,128)(2,1)} %param.10) | copy-start | bytes 1572868
  7.2 19.5 %copy-start.1 = (bf16[1024,512]{1,0:T(8,128)(2,1)S(1)}, bf16[1024,512]{1,0:T(8,128)(2,1)}, u32[]{:S(2)}) copy-start(bf16[1024,512]{1,0:T(8,128)(2,1)} %param.11) | copy-start | bytes 3145732
  7.2 73.1 %all-gather.3.cloned.1.call-start = ((), (), s32[]{:S(2)}) async-start(), calls=%async_computation.4 | async-start | bytes 2228224 | tf_op jit(solution)/shard_map/all_gather | solution.py:163
  11.1 27.7 %copy-start.32 = (s32[384]{0:T(512)}, s32[384]{0:T(512)S(1)}, u32[]{:S(2)}) copy-start(s32[384]{0:T(512)S(1)} %reduce.4) | copy-start | bytes 4612
  14.9 13.9 %all-to-all-start = ((s32[16,1,48]{2,1,0:T(1,128)}), s32[16,1,48]{2,1,0:T(1,128)S(1)}, u32[]{:S(2)}, u32[]{:S(2)}) async-start(s32[16,1,48]{2,1,0:T(1,128)} %all_to_all.12), calls=%async_computation | async-start | bytes 16384 | tf_op jit(solution)/shard_map/all_to_all | solution.py:181
  26.6 6.2 copy-start.42
  27.0 58.6 %copy-start.37 = (s32[384]{0:T(512)}, s32[384]{0:T(512)S(1)}, u32[]{:S(2)}) copy-start(s32[384]{0:T(512)S(1)} %convert_reduce_fusion) | copy-start | bytes 4612
  30.1 2.7 copy-start.27
  32.9 6.0 copy-start.43
  33.9 17.0 %all-to-all-start.1 = ((bf16[16,48,512]{2,1,0:T(8,128)(2,1)}), bf16[16,48,512]{2,1,0:T(8,128)(2,1)S(1)}, u32[]{:S(2)}, u32[]{:S(2)}) async-start(bf16[16,48,512]{2,1,0:T(8,128)(2,1)} %broadcast_select_fusion), calls=%async_computation.1 | async-start | bytes 1572864 | tf_op jit(solution)/shard_map/all_to_all | solution.py:186
  38.8 101.4 %all-gather.5.cloned.1.call-start = ((), (), s32[]{:S(2)}) async-start(), calls=%async_computation.5 | async-start | bytes 1114112 | tf_op jit(solution)/shard_map/all_gather | solution.py:190
  39.5 40.8 %copy-start.34 = (f32[384]{0:T(512)}, f32[384]{0:T(512)S(1)}, u32[]{:S(2)}) copy-start(f32[384]{0:T(512)S(1)} %get-tuple-element.12) | copy-start | bytes 4612
  40.2 40.1 %copy-start.9 = (bf16[384,512]{1,0:T(8,128)(2,1)S(1)}, bf16[384,512]{1,0:T(8,128)(2,1)}, u32[]{:S(2)}) copy-start(bf16[384,512]{1,0:T(8,128)(2,1)} %param.8) | copy-start | bytes 1179652
  41.0 322.0 %all-reduce.4.cloned.1.call-start = ((), (), s32[]{:S(2)}) async-start(), calls=%async_computation.6 | async-start | bytes 2097152 | tf_op jit(solution)/shard_map/psum | solution.py:222
  84.8 4.4 copy-start.2
  85.0 2.2 copy-start.22
  85.3 1.9 copy-start.24
  85.6 1.6 copy-start.25
  87.2 2.4 copy-start.13
  87.2 2.4 copy-start.15
  87.3 2.4 copy-start.17
  87.3 2.4 copy-start.19
  87.3 1.9 copy-start.10
  88.3 2.1 copy-start.8
  88.4 2.1 copy-start.41
  89.7 52.5 %copy-start.5 = (f32[384,512]{1,0:T(8,128)}, f32[384,512]{1,0:T(8,128)S(1)}, u32[]{:S(2)}) copy-start(f32[384,512]{1,0:T(8,128)S(1)} %get-tuple-element.25) | copy-start | bytes 2359300
  140.2 2.0 copy-start.31
  140.2 2.1 copy-start.21
  142.2 1.4 copy-start.6
  142.2 1.4 copy-start.29
  142.2 1.4 copy-start.39
  142.3 1.4 copy-start.36
  143.7 1.6 copy-start.3
  146.6 2.2 copy-start.30
  152.1 6.9 copy-start.28
  154.5 214.0 %all-to-all-start.2 = ((bf16[16,48,512]{2,1,0:T(8,128)(2,1)}), bf16[16,48,512]{2,1,0:T(8,128)(2,1)}, u32[]{:S(2)}, u32[]{:S(2)}) async-start(bf16[16,48,512]{2,1,0:T(8,128)(2,1)} %bitcast.58), calls=%async_computation.2 | async-start | bytes 1572864 | tf_op jit(solution)/shard_map/all_to_all | solution.py:201
  159.0 295.3 %reduce-scatter.2.cloned.1.call-start = ((), (), s32[]{:S(2)}) async-start(), calls=%async_computation.8 | async-start | bytes 1114112 | tf_op jit(solution)/shard_map/reduce_scatter | solution.py:213
  159.0 2.6 copy-start.26
  161.6 1.4 copy-start.38
  161.6 1.4 copy-start.44
  163.0 2.2 copy-start.20
  163.0 3.2 copy-start.18
  163.0 4.1 copy-start.16
  163.0 5.1 copy-start.14
  165.2 4.0 copy-start.7
  165.2 4.0 copy-start.40
  171.0 404.1 %all-reduce.6.cloned.1.call-start = ((), (), s32[]{:S(2)}) async-start(), calls=%async_computation.7 | async-start | bytes 2097152 | tf_op jit(solution)/shard_map/psum | solution.py:222
  175.0 3.4 copy-start.23
  178.5 3.3 copy-start.12
  179.8 183.2 %copy-start.11 = (bf16[384,512]{1,0:T(8,128)(2,1)S(1)}, bf16[384,512]{1,0:T(8,128)(2,1)}, u32[]{:S(2)}) copy-start(bf16[384,512]{1,0:T(8,128)(2,1)} %param.8) | copy-start | bytes 1179652
  363.0 428.0 %all-reduce.8.cloned.1.call-start = ((), (), s32[]{:S(2)}) async-start(), calls=%async_computation.9 | async-start | bytes 2097152 | tf_op jit(solution)/shard_map/psum | solution.py:220
  458.4 2.8 copy-start.33
  458.4 2.8 copy-start.35
  791.0 1.7 copy-start.4
Sparse Core Ops, SparseCore 0:
  11.0 69.2 all-gather.2
  83.3 56.8 all-gather.4
  148.9 214.0 all-reduce.3
  366.9 87.3 reduce-scatter.1
  457.4 117.7 all-reduce.5
  577.3 213.6 all-reduce.7
